TPU v7x, 256 devices: a whole 4x4x8 slice. The times are simulated.
256 devices in a mesh: group: 8 (over z_lo, y), ctx: 32 (over x, z_hi, core).
Axes of the slice: x: 4, y: 4, z: 8 (z_hi: 4, z_lo: 2; z = z_hi * 2 + z_lo), core: 2. Of those that a mesh axis runs over, the one named last changes fastest.
Arguments:
- hidden_x: bfloat16 [8, 8192, 8192], P('group', 'ctx'), may hold values from -6 to 6
- gate_z: bfloat16 [8, 8192, 8192], P('group', 'ctx'), may hold values from -6 to 6
- lengths: int32 [8, 32], P('group', 'ctx'), may hold values from 128 to 256, as said below
- conv_weight: float32 [4, 8192], P(None, ('group', 'ctx')), may hold values from -3 to 3
- conv_bias: float32 [8192], P(('group', 'ctx')), may hold values from -3 to 3
- xproj_weight: bfloat16 [8192, 288], P(('group', 'ctx')), may hold values from -0.0625 to 0.0625
- dtproj_weight: bfloat16 [256, 8192], P(None, ('group', 'ctx')), may hold values from -0.375 to 0.375
- dt_bias: float32 [8192], P(('group', 'ctx')), may hold values from -4.6 to -2.25
- a_log: float32 [16, 8192], P(None, ('group', 'ctx')), may hold values from -8.5 to -0.7
- skip_gain: float32 [8192], P(('group', 'ctx')), may hold values from 0.5 to 2
Outputs:
- gated: bfloat16 [8, 8192, 8192], P('group', 'ctx')
Inputs may be any that keep to these rules, and one draw needn't show every extreme that they name: Block c of record r holds lengths[r, c] valid positions at its start and padding after them.
All inputs are finite; a program needn't handle non-finite values.
Results may differ from a plain program's by a relative error of at most 0.0015.
The roundings to bfloat16 on the way count: a program that leaves them out, or rounds other values in their place, can miss the bound.
Values may be sent and summed in bfloat16 or wider, within the bound.
No kernel may reach another device: no remote copies, remote signals or barrier semaphores. Data moves between devices by JAX's collectives and lax.ppermute only.
A program may use at most 192 MiB of HBM per device.

v0:
```python
import jax
import jax.numpy as jnp
from jax import lax
from jax.sharding import PartitionSpec as P


def shifted(block, axis, distance):
    devices = range(lax.axis_size(axis))
    route = [(i - distance, i) for i in devices if i - distance in devices]
    return lax.ppermute(block, axis, route)


def run_scan(state, x_act, step_size, b_rows, c_rows, a_matrix):
    tok_rows, width = x_act.shape
    blocks = tok_rows // 16

    def advance(state, block):
        x_block, d_block, b_block, c_block = block
        outputs = []
        for offset in range(16):
            state = (
                jnp.exp(a_matrix * d_block[offset][None, :]) * state
                + (d_block[offset] * x_block[offset])[None, :] * b_block[offset][:, None]
            )
            outputs.append(jnp.sum(c_block[offset][:, None] * state, axis=0))
        return (state, jnp.stack(outputs))

    ending, y_blocks = lax.scan(
        advance,
        state,
        (
            x_act.reshape(blocks, 16, width),
            step_size.reshape(blocks, 16, width),
            b_rows.reshape(blocks, 16, -1),
            c_rows.reshape(blocks, 16, -1),
        ),
    )
    return (y_blocks.reshape(tok_rows, width), ending)


def shards(
    hidden_x,
    gate_z,
    lengths,
    conv_weight,
    conv_bias,
    xproj_weight,
    dtproj_weight,
    dt_bias,
    a_log,
    skip_gain,
):
    tok_rows = hidden_x.shape[1]
    taps = conv_weight.shape[0]
    valid_row = (lax.iota(jnp.int32, tok_rows) < lengths[0, 0]).astype(jnp.float32)
    valid = valid_row[:, None]
    conv_full, bias_full, dtb_full, alog_full, skip_full = (
        lax.all_gather(conv_weight, ("group", "ctx"), axis=1, tiled=True),
        lax.all_gather(conv_bias, ("group", "ctx"), axis=0, tiled=True),
        lax.all_gather(dt_bias, ("group", "ctx"), axis=0, tiled=True),
        lax.all_gather(a_log, ("group", "ctx"), axis=1, tiled=True),
        lax.all_gather(skip_gain, ("group", "ctx"), axis=0, tiled=True),
    )
    masked_half = hidden_x[0] * valid_row.astype(jnp.bfloat16)[:, None]
    rim_rows = shifted(masked_half[tok_rows - (taps - 1) :], "ctx", 1)
    padded = jnp.concatenate(
        [rim_rows.astype(jnp.float32), masked_half.astype(jnp.float32)], axis=0
    )
    total = bias_full[None, :] + conv_full[0][None, :] * padded[0:tok_rows]
    for offset in range(1, taps):
        total = total + conv_full[offset][None, :] * padded[offset : offset + tok_rows]
    conv_act = jax.nn.silu(total).astype(jnp.bfloat16)
    rank = dtproj_weight.shape[0]
    states = alog_full.shape[0]
    proj = jnp.dot(
        conv_act,
        lax.all_gather(xproj_weight, ("group", "ctx"), axis=0, tiled=True),
        preferred_element_type=jnp.float32,
    )
    dt_low = proj[:, :rank].astype(jnp.bfloat16)
    b_rows = proj[:, rank : rank + states]
    c_rows = proj[:, rank + states :]
    step_size = (
        jax.nn.softplus(
            jnp.dot(
                dt_low,
                lax.all_gather(dtproj_weight, ("group", "ctx"), axis=1, tiled=True),
                preferred_element_type=jnp.float32,
            )
            + dtb_full[None, :]
        )
        * valid
    )
    a_matrix = -jnp.exp(alog_full)
    x_act = conv_act.astype(jnp.float32)
    zero_state = jnp.zeros(a_matrix.shape, jnp.float32)
    y_local, local_end = run_scan(zero_state, x_act, step_size, b_rows, c_rows, a_matrix)
    total_decay = jnp.exp(a_matrix * jnp.sum(step_size, axis=0)[None, :])

    def relay(turn, incoming):
        return shifted(total_decay * incoming + local_end, "ctx", 1)

    incoming = lax.fori_loop(0, lax.axis_size("ctx") - 1, relay, zero_state)
    y_all, ending = run_scan(incoming, x_act, step_size, b_rows, c_rows, a_matrix)
    mixed = (
        (y_all + skip_full[None, :] * x_act) * jax.nn.silu(gate_z[0].astype(jnp.float32)) * valid
    )
    return mixed.astype(jnp.bfloat16)[None]


def solution(mesh):
    in_specs = (
        P("group", "ctx", None),
        P("group", "ctx", None),
        P("group", "ctx"),
        P(None, ("group", "ctx")),
        P(("group", "ctx")),
        P(("group", "ctx"), None),
        P(None, ("group", "ctx")),
        P(("group", "ctx")),
        P(None, ("group", "ctx")),
        P(("group", "ctx")),
    )
    out_specs = P("group", "ctx", None)
    return jax.shard_map(shards, mesh=mesh, in_specs=in_specs, out_specs=out_specs, check_vma=False)
```

profile of v0, /device:TPU:18, one launch (start us, length us, event | category | flops | bytes accessed | tf_op | source)
XLA Modules:
  0.0 1949.0 jit_solution(5807592894544555180)
XLA Ops:
  11.9 6.3 fusion.89
  20.2 331.3 %all-gather.1 = f32[256,32,4]{1,2,0:T(4,128)S(1)} all-gather(f32[1,32,4]{1,2,0:T(4,128)S(1)} %bitcast.520), channel_id=1, replica_groups=mesh['group'=8,'ctx'=32] {'group','ctx'}, dimensions={0}, use_global_device_ids=true | all-gather | bytes 131584 | tf_op jit(solution)/shard_map/all_gather | solution.py:58
  351.8 403.9 %all-gather = f32[256,32,16]{1,2,0:T(8,128)S(1)} all-gather(f32[1,32,16]{1,2,0:T(8,128)S(1)} %bitcast.519), channel_id=1, replica_groups=mesh['group'=8,'ctx'=32] {'group','ctx'}, dimensions={0}, use_global_device_ids=true | all-gather | bytes 526336 | tf_op jit(solution)/shard_map/all_gather | solution.py:61
  761.7 13.6 multiply_convert_fusion
  781.6 6.3 fusion.93
  788.2 299.0 %all-gather.7.cloned.1.call-done = bf16[256,8192]{0,1:T(8,128)(2,1)} async-done(((bf16[256,32]{0,1:T(8,128)(2,1)}), bf16[256,8192]{0,1:T(8,128)(2,1)}) %all-gather.7.cloned.1.call-update) | async-done | bytes 4194320 | tf_op jit(solution)/shard_map/all_gather | solution.py:87
  1087.2 10.6 fusion.92
  1097.8 118.0 %while.35 = (s32[]{:T(128)}, f32[16,8192]{1,0:T(8,128)S(1)}, f32[16,16,8192]{2,1,0:T(8,128)}, f32[16,8192]{1,0:T(8,128)S(1)}, f32[16,16,8192]{2,1,0:T(8,128)}, /...) while((s32[]{:T(128)}, f32[16,8192]{1,0:T(8,128)S(1)}, ...), condition=%wide.region_2.3_spmd.clone, body=%wide.region_1.2_spmd.clone.sunk | while | flops 8650770 | bytes 6295059 | solution.py:28
  1097.9 5.1 constant_dynamic-slice_fusion.115
  1105.3 5.2 constant_dynamic-slice_fusion.115
  1119.9 5.1 constant_dynamic-slice_fusion.115
  1141.9 5.3 constant_dynamic-slice_fusion.115
  1156.5 5.1 constant_dynamic-slice_fusion.115
  1171.0 5.3 constant_dynamic-slice_fusion.115
  1178.6 5.3 constant_dynamic-slice_fusion.115
  1193.3 5.4 constant_dynamic-slice_fusion.115
  1200.9 5.3 constant_dynamic-slice_fusion.115
  1208.5 5.3 constant_dynamic-slice_fusion.115
  1215.9 514.3 %while.33 = (s32[]{:T(128)}, f32[16,8192]{1,0:T(8,128)S(1)}, f32[16,8192]{1,0:T(8,128)S(1)}, f32[16,8192]{1,0:T(8,128)S(1)}, s32[]{:T(128)}) while((s32[]{:T(128)}, f32[16,8192]{1,0:T(8,128)S(1)}, f32[16,8192]{1,0:T(8,128)S(1)}, f32[16,8192]{1,0:T(8,128)S(1)}, s32[]{:T(128)}) %tuple.251), condition=%wide.region_4.5_spmd, body=%wide.region_3.4_spmd.sunk | while | flops 262146 | bytes 4194405 | solution.py:103
  1217.9 16.6 collective-permute-done
  1236.6 13.6 collective-permute-done
  1252.2 14.8 collective-permute-done
  1268.9 15.6 collective-permute-done
  1286.6 12.7 collective-permute-done
  1301.3 14.5 collective-permute-done
  1317.8 14.5 collective-permute-done
  1334.4 14.7 collective-permute-done
  1351.0 14.5 collective-permute-done
  1367.6 14.5 collective-permute-done
  1384.1 14.7 collective-permute-done
  1400.8 14.5 collective-permute-done
  1417.3 14.5 collective-permute-done
  1433.8 14.7 collective-permute-done
  1450.5 14.5 collective-permute-done
  1467.1 14.5 collective-permute-done
  1483.6 14.7 collective-permute-done
  1500.3 14.5 collective-permute-done
  1516.8 14.5 collective-permute-done
  1533.3 14.7 collective-permute-done
  1550.0 14.5 collective-permute-done
  1566.6 14.5 collective-permute-done
  1583.1 14.7 collective-permute-done
  1599.8 14.5 collective-permute-done
  1616.3 14.5 collective-permute-done
  1632.8 14.7 collective-permute-done
  1649.5 14.5 collective-permute-done
  1666.0 14.5 collective-permute-done
  1682.6 14.7 collective-permute-done
  1699.3 14.5 collective-permute-done
  1715.8 14.4 collective-permute-done
  1730.2 203.4 %while.34 = (s32[]{:T(128)}, f32[16,8192]{1,0:T(8,128)S(1)}, f32[16,16,8192]{2,1,0:T(8,128)}, f32[16,16,8192]{2,1,0:T(8,128)}, f32[16,8192]{1,0:T(8,128)S(1)}, /...) while((s32[]{:T(128)}, f32[16,8192]{1,0:T(8,128)S(1)}, ...), condition=%wide.region_22.23_spmd, body=%wide.region_5.22_spmd.sunk | while | flops 18874384 | bytes 15473949 | solution.py:28
  1730.3 5.2 constant_dynamic-slice_fusion.114
  1742.9 5.3 constant_dynamic-slice_fusion.114
  1768.2 5.2 constant_dynamic-slice_fusion.114
  1780.9 5.1 constant_dynamic-slice_fusion.114
  1793.5 5.2 constant_dynamic-slice_fusion.114
  1806.2 5.3 constant_dynamic-slice_fusion.114
  1831.4 5.2 constant_dynamic-slice_fusion.114
  1856.7 5.4 constant_dynamic-slice_fusion.114
  1869.6 5.4 constant_dynamic-slice_fusion.114
  1895.0 5.5 constant_dynamic-slice_fusion.114
  1908.0 5.4 constant_dynamic-slice_fusion.114
  1920.8 5.4 constant_dynamic-slice_fusion.114
  1933.6 8.8 fusion.87
  (795 shorter events, 281.2 us)
Async XLA Ops:
  6.5 755.2 %all-reduce.6.cloned.1.call-start = ((), (), s32[]{:S(2)}) async-start(), calls=%async_computation.2 | async-start | bytes 196608
  7.4 1.7 copy-start.2
  8.2 0.9 copy-start.3
  9.1 0.6 copy-start.1
  9.7 771.9 %all-gather.5.cloned.1.call-start = ((), (), s32[]{:S(2)}) async-start(), calls=%async_computation | async-start | bytes 6316032 | tf_op jit(solution)/shard_map/all_gather | solution.py:77
  10.5 1076.7 %all-gather.7.cloned.1.call-start = ((), (), s32[]{:S(2)}) async-start(), calls=%async_computation.1 | async-start | bytes 4210688 | tf_op jit(solution)/shard_map/all_gather | solution.py:87
  11.9 8.3 copy-start.6
  11.9 339.9 %copy-start.5 = (f32[16,32]{1,0:T(8,128)S(1)}, f32[16,32]{1,0:T(8,128)}, u32[]{:S(2)}) copy-start(f32[16,32]{1,0:T(8,128)} %param.24) | copy-start | bytes 6148
  18.2 743.4 %collective-permute-start.1 = (bf16[3,8192]{1,0:T(4,128)(2,1)S(1)}, bf16[3,8192]{1,0:T(4,128)(2,1)S(1)}, u32[]{:S(2)}, u32[]{:S(2)}) collective-permute-start(bf16[3,8192]{1,0:T(4,128)(2,1)S(1)} %slice.574), channel_id=1, source_target_pairs={{0,1},{1,2},{2,3},{3,4},{4,5},{5,6},{6,7},{7,8},{8,9},{9,10},{10,1... | collective-permute-start | bytes 147464 | tf_op jit(solution)/shard_map/ppermute | solution.py:10
  775.4 2.0 copy-start
  781.6 305.6 %copy-start.7 = (f32[8192]{0:T(1024)S(1)}, f32[8192]{0:T(1024)}, u32[]{:S(2)}) copy-start(f32[8192]{0:T(1024)} %get-tuple-element.232) | copy-start | bytes 98308
  1216.0 18.6 collective-permute-start
  1234.6 15.5 collective-permute-start
  1250.2 16.7 collective-permute-start
  1267.0 17.6 collective-permute-start
  1284.6 14.6 collective-permute-start
  1299.3 16.5 collective-permute-start
  1315.9 16.5 collective-permute-start
  1332.4 16.6 collective-permute-start
  1349.1 16.5 collective-permute-start
  1365.6 16.5 collective-permute-start
  1382.2 16.6 collective-permute-start
  1398.8 16.5 collective-permute-start
  1415.4 16.5 collective-permute-start
  1431.9 16.6 collective-permute-start
  1448.6 16.5 collective-permute-start
  1465.1 16.5 collective-permute-start
  1481.7 16.6 collective-permute-start
  1498.3 16.5 collective-permute-start
  1514.9 16.5 collective-permute-start
  1531.4 16.6 collective-permute-start
  1548.1 16.5 collective-permute-start
  1564.6 16.5 collective-permute-start
  1581.2 16.6 collective-permute-start
  1597.8 16.5 collective-permute-start
  1614.4 16.5 collective-permute-start
  1630.9 16.6 collective-permute-start
  1647.6 16.5 collective-permute-start
  1664.1 16.5 collective-permute-start
  1680.7 16.6 collective-permute-start
  1697.3 16.5 collective-permute-start
  1713.9 16.4 collective-permute-start
  1730.2 203.4 %copy-start.4 = (f32[8192]{0:T(1024)S(1)}, f32[8192]{0:T(1024)}, u32[]{:S(2)}) copy-start(f32[8192]{0:T(1024)} %get-tuple-element.234) | copy-start | bytes 98308
Sparse Core Ops, SparseCore 0:
  13.4 244.1 all-reduce.5
  259.4 414.3 all-gather.4
  675.7 411.3 all-gather.6
where the time goes:
time: 1950 us
  waiting for transfers between devices  752 us (39%)
  blocking collectives  735 us (38%)
  local copies, waits for them, and re-layouts  206 us (11%)
  other arithmetic  157 us (8%)
  starting transfers between devices  61.5 us (3%)
    ppermute x32, waiting for transfers between devices, shifted(): return lax.ppermute(block, axis, route)  452 us
    all_gather x1, blocking collectives, shards(): lax.all_gather(a_log, ('group', 'ctx'), axis=1, tiled=True)  404 us
    all_gather x1, blocking collectives, shards(): lax.all_gather(conv_weight, ('group', 'ctx'), axis=1, tiled=True)  331 us
    all_gather x1, waiting for transfers between devices, shards(): lax.all_gather(dtproj_weight, ('group', 'ctx'), axis=1, tiled=True)  299 us
    slice x32, local copies, waits for them, and re-layouts, advance(): x_block[offset]  167 us
    reduce_sum x80, other arithmetic, advance(): outputs.append(jnp.sum(c_block[offset][:, None] * state, axis=0))  88.3 us
    ppermute x32, starting transfers between devices, shifted(): return lax.ppermute(block, axis, route)  61.5 us
  transfers between devices with their start and end apart: 35, of which 32 were waited for; matrix products, arithmetic and copies ran while one was open for 2% of the time, Pallas kernels for 0%

commit v1 on v0

--- a/solution.py
+++ b/solution.py
@@ -84,7 +84,15 @@
         jax.nn.softplus(
             jnp.dot(
                 dt_low,
-                lax.all_gather(dtproj_weight, ("group", "ctx"), axis=1, tiled=True),
+                jnp.concatenate(
+                    lax.all_to_all(
+                        jnp.stack([dtproj_weight] * lax.axis_size(("group", "ctx"))),
+                        ("group", "ctx"),
+                        0,
+                        0,
+                    ),
+                    axis=1,
+                ),
                 preferred_element_type=jnp.float32,
             )
             + dtb_full[None, :]

time: 1950 us -> 1780 us (0.913)
  the two profiles are of different devices: /device:TPU:18 before, /device:TPU:30 now
where the time goes in v1:
time: 1780 us
  blocking collectives  870 us (49%)
  waiting for transfers between devices  427 us (24%)
  local copies, waits for them, and re-layouts  212 us (12%)
  other arithmetic  157 us (9%)
  starting transfers between devices  77.2 us (4%)
    all_gather x1, blocking collectives, shards(): lax.all_gather(conv_weight, ('group', 'ctx'), axis=1, tiled=True)  464 us
    ppermute x32, waiting for transfers between devices, shifted(): return lax.ppermute(block, axis, route)  426 us
    all_gather x1, blocking collectives, shards(): lax.all_gather(a_log, ('group', 'ctx'), axis=1, tiled=True)  405 us
    slice x32, local copies, waits for them, and re-layouts, advance(): x_block[offset]  169 us
    reduce_sum x80, other arithmetic, advance(): outputs.append(jnp.sum(c_block[offset][:, None] * state, axis=0))  88.3 us
    ppermute x32, starting transfers between devices, shifted(): return lax.ppermute(block, axis, route)  61.7 us
  transfers between devices with their start and end apart: 35, of which 31 were waited for; matrix products, arithmetic and copies ran while one was open for 2% of the time, Pallas kernels for 0%

profile of v1, /device:TPU:30, one launch (start us, length us, event | category | flops | bytes accessed | tf_op | source)
XLA Modules:
  0.0 1779.3 jit_solution(4070028302417056029)
XLA Ops:
  13.8 15.4 all-to-all-start
  29.9 6.3 fusion.89
  38.3 464.5 %all-gather.1 = f32[256,32,4]{1,2,0:T(4,128)S(1)} all-gather(f32[1,32,4]{1,2,0:T(4,128)S(1)} %bitcast.523), channel_id=1, replica_groups=mesh['group'=8,'ctx'=32] {'group','ctx'}, dimensions={0}, use_global_device_ids=true | all-gather | bytes 131584 | tf_op jit(solution)/shard_map/all_gather | solution.py:58
  503.1 405.2 %all-gather = f32[256,32,16]{1,2,0:T(8,128)S(1)} all-gather(f32[1,32,16]{1,2,0:T(8,128)S(1)} %bitcast.522), channel_id=1, replica_groups=mesh['group'=8,'ctx'=32] {'group','ctx'}, dimensions={0}, use_global_device_ids=true | all-gather | bytes 526336 | tf_op jit(solution)/shard_map/all_gather | solution.py:61
  914.4 13.1 multiply_convert_fusion
  933.5 6.3 fusion.93
  940.1 10.6 fusion.92
  950.8 120.6 %while.35 = (s32[]{:T(128)}, f32[16,8192]{1,0:T(8,128)S(1)}, f32[16,16,8192]{2,1,0:T(8,128)}, f32[16,8192]{1,0:T(8,128)S(1)}, f32[16,16,8192]{2,1,0:T(8,128)}, /...) while((s32[]{:T(128)}, f32[16,8192]{1,0:T(8,128)S(1)}, ...), condition=%wide.region_2.3_spmd.clone, body=%wide.region_1.2_spmd.clone.sunk | while | flops 8650770 | bytes 6295059 | solution.py:28
  950.9 5.2 constant_dynamic-slice_fusion.115
  958.3 5.2 constant_dynamic-slice_fusion.115
  965.8 5.2 constant_dynamic-slice_fusion.115
  973.2 5.7 constant_dynamic-slice_fusion.115
  981.2 5.3 constant_dynamic-slice_fusion.115
  988.8 5.3 constant_dynamic-slice_fusion.115
  996.3 5.4 constant_dynamic-slice_fusion.115
  1011.3 5.4 constant_dynamic-slice_fusion.115
  1033.8 5.4 constant_dynamic-slice_fusion.115
  1041.4 5.4 constant_dynamic-slice_fusion.115
  1049.1 5.4 constant_dynamic-slice_fusion.115
  1071.4 488.6 %while.33 = (s32[]{:T(128)}, f32[16,8192]{1,0:T(8,128)S(1)}, f32[16,8192]{1,0:T(8,128)S(1)}, f32[16,8192]{1,0:T(8,128)S(1)}, s32[]{:T(128)}) while((s32[]{:T(128)}, f32[16,8192]{1,0:T(8,128)S(1)}, f32[16,8192]{1,0:T(8,128)S(1)}, f32[16,8192]{1,0:T(8,128)S(1)}, s32[]{:T(128)}) %tuple.251), condition=%wide.region_4.5_spmd, body=%wide.region_3.4_spmd.sunk | while | flops 262146 | bytes 4194405 | solution.py:111
  1073.6 15.9 collective-permute-done
  1091.5 15.2 collective-permute-done
  1108.7 14.3 collective-permute-done
  1124.9 14.3 collective-permute-done
  1141.2 14.4 collective-permute-done
  1157.7 15.0 collective-permute-done
  1174.7 14.3 collective-permute-done
  1191.0 14.4 collective-permute-done
  1207.4 15.0 collective-permute-done
  1224.4 14.3 collective-permute-done
  1240.7 14.4 collective-permute-done
  1257.2 15.0 collective-permute-done
  1274.2 14.3 collective-permute-done
  1290.5 14.4 collective-permute-done
  1306.9 15.0 collective-permute-done
  1323.9 14.3 collective-permute-done
  1340.2 14.4 collective-permute-done
  1356.7 15.0 collective-permute-done
  1373.7 14.3 collective-permute-done
  1390.0 14.4 collective-permute-done
  1406.4 15.0 collective-permute-done
  1423.4 14.3 collective-permute-done
  1439.7 11.6 collective-permute-done
  1453.3 11.6 collective-permute-done
  1466.9 11.6 collective-permute-done
  1480.5 11.6 collective-permute-done
  1494.1 11.6 collective-permute-done
  1507.6 11.6 collective-permute-done
  1521.2 11.6 collective-permute-done
  1534.8 11.6 collective-permute-done
  1548.4 11.6 collective-permute-done
  1560.0 203.7 %while.34 = (s32[]{:T(128)}, f32[16,8192]{1,0:T(8,128)S(1)}, f32[16,16,8192]{2,1,0:T(8,128)}, f32[16,16,8192]{2,1,0:T(8,128)}, f32[16,8192]{1,0:T(8,128)S(1)}, /...) while((s32[]{:T(128)}, f32[16,8192]{1,0:T(8,128)S(1)}, ...), condition=%wide.region_22.23_spmd, body=%wide.region_5.22_spmd.sunk | while | flops 18874384 | bytes 15473949 | solution.py:28
  1560.0 5.2 constant_dynamic-slice_fusion.114
  1572.6 5.2 constant_dynamic-slice_fusion.114
  1585.2 5.2 constant_dynamic-slice_fusion.114
  1597.9 5.7 constant_dynamic-slice_fusion.114
  1611.1 5.3 constant_dynamic-slice_fusion.114
  1623.8 5.3 constant_dynamic-slice_fusion.114
  1636.6 5.4 constant_dynamic-slice_fusion.114
  1662.0 5.4 constant_dynamic-slice_fusion.114
  1700.0 5.4 constant_dynamic-slice_fusion.114
  1712.9 5.4 constant_dynamic-slice_fusion.114
  1725.7 5.4 constant_dynamic-slice_fusion.114
  1763.7 8.8 fusion.87
  (795 shorter events, 285.3 us)
Async XLA Ops:
  6.5 907.8 %all-reduce.6.cloned.1.call-start = ((), (), s32[]{:S(2)}) async-start(), calls=%async_computation.2 | async-start | bytes 196608
  7.4 1.7 copy-start.2
  8.2 0.9 copy-start.3
  9.1 0.6 copy-start.1
  9.8 923.8 %all-gather.4.cloned.1.call-start = ((), (), s32[]{:S(2)}) async-start(), calls=%async_computation.1 | async-start | bytes 6316032 | tf_op jit(solution)/shard_map/all_gather | solution.py:77
  13.8 926.3 %all-to-all-start = ((bf16[256,256,32]{1,2,0:T(8,128)(2,1)}), bf16[256,256,32]{1,2,0:T(8,128)(2,1)}, u32[]{:S(2)}, u32[]{:S(2)}) async-start(bf16[256,256,32]{1,2,0:T(8,128)(2,1)} %stack.36), calls=%async_computation | async-start | bytes 8388608 | tf_op jit(solution)/shard_map/all_to_all | solution.py:88
  29.8 8.5 copy-start.6
  29.8 473.2 %copy-start.5 = (f32[16,32]{1,0:T(8,128)S(1)}, f32[16,32]{1,0:T(8,128)}, u32[]{:S(2)}) copy-start(f32[16,32]{1,0:T(8,128)} %param.24) | copy-start | bytes 6148
  36.2 878.1 %collective-permute-start.1 = (bf16[3,8192]{1,0:T(4,128)(2,1)S(1)}, bf16[3,8192]{1,0:T(4,128)(2,1)S(1)}, u32[]{:S(2)}, u32[]{:S(2)}) collective-permute-start(bf16[3,8192]{1,0:T(4,128)(2,1)S(1)} %slice.574), channel_id=1, source_target_pairs={{0,1},{1,2},{2,3},{3,4},{4,5},{5,6},{6,7},{7,8},{8,9},{9,10},{10,1... | collective-permute-start | bytes 147464 | tf_op jit(solution)/shard_map/ppermute | solution.py:10
  927.4 2.0 copy-start
  933.5 6.5 copy-start.7
  1071.5 18.0 %collective-permute-start = (f32[16,8192]{1,0:T(8,128)S(1)}, f32[16,8192]{1,0:T(8,128)S(1)}, u32[]{:S(2)}, u32[]{:S(2)}) collective-permute-start(f32[16,8192]{1,0:T(8,128)S(1)} %multiply_add_fusion.24), channel_id=1, source_target_pairs={{0,1},{1,2},{2,3},{3,4},{4,5},{5,6},{6,7},{7,8},{8,9},{9,10},{10,1... | collective-permute-start | bytes 1572872 | tf_op jit(solution)/shard_map/while/body/eval_jaxpr/ppermute | solution.py:10
  1089.5 17.1 collective-permute-start
  1106.7 16.2 collective-permute-start
  1123.0 16.2 collective-permute-start
  1139.3 16.4 collective-permute-start
  1155.8 16.9 collective-permute-start
  1172.7 16.2 collective-permute-start
  1189.0 16.4 collective-permute-start
  1205.5 16.9 collective-permute-start
  1222.5 16.2 collective-permute-start
  1238.8 16.4 collective-permute-start
  1255.3 16.9 collective-permute-start
  1272.2 16.2 collective-permute-start
  1288.5 16.4 collective-permute-start
  1305.0 16.9 collective-permute-start
  1322.0 16.2 collective-permute-start
  1338.3 16.4 collective-permute-start
  1354.7 16.9 collective-permute-start
  1371.7 16.2 collective-permute-start
  1388.0 16.4 collective-permute-start
  1404.5 16.9 collective-permute-start
  1421.5 16.2 collective-permute-start
  1437.8 13.5 collective-permute-start
  1451.4 13.5 collective-permute-start
  1465.0 13.5 collective-permute-start
  1478.5 13.5 collective-permute-start
  1492.1 13.5 collective-permute-start
  1505.7 13.5 collective-permute-start
  1519.3 13.5 collective-permute-start
  1532.9 13.5 collective-permute-start
  1546.5 13.5 collective-permute-start
  1560.0 203.7 %copy-start.4 = (f32[8192]{0:T(1024)S(1)}, f32[8192]{0:T(1024)}, u32[]{:S(2)}) copy-start(f32[8192]{0:T(1024)} %get-tuple-element.234) | copy-start | bytes 98308
Sparse Core Ops, SparseCore 0:
  13.4 259.0 all-reduce.5
  274.4 412.0 all-gather.3
